TPU v7x, 128 devices: a whole 4x4x4 slice. The times are simulated.
128 devices in a mesh: px: 8 (over y, core), py: 16 (over x, z).
Axes of the slice: x: 4, y: 4, z: 4, core: 2. Of those that a mesh axis runs over, the one named last changes fastest.
Arguments:
- initial_trace: float32 [80, 256, 2048], P(None, 'px', 'py'), may hold values from -6 to 6
- trace_rhs: float32 [80, 256, 2048], P(None, 'px', 'py'), may hold values from -6 to 6
- face_scale: float32 [256, 2048], P('px', 'py'), may hold values from 0.5 to 2
- block_inverse: float32 [80, 80], replicated, as said below
- coupling: float32 [4, 80, 80], replicated, may hold values from -0.078125 to 0.078125
- element_state: bfloat16 [320, 256, 2048], P(None, 'px', 'py'), may hold values from -6 to 6
- recover_self: bfloat16 [640, 320], replicated, may hold values from -0.25 to 0.25
- recover_faces: bfloat16 [5, 640, 80], replicated, may hold values from -0.3125 to 0.3125
- residual_map: bfloat16 [640, 640], replicated, may hold values from -0.25 to 0.25
- error_map: bfloat16 [640, 320], replicated, may hold values from -0.3125 to 0.3125
- raise_map: bfloat16 [640, 320], replicated, may hold values from -0.3125 to 0.3125
- raise_flag: int32 [256, 2048], P('px', 'py'), may hold values from 0 to 1, as said below
- new_owner: int32 [256, 2048], P('px', 'py'), may hold values from 0 to 127, as said below
Outputs:
- final_trace: float32 [80, 256, 2048], P(None, 'px', 'py')
- indicator: float32 [256, 2048], P('px', 'py')
- raised_state: bfloat16 [640, 262144], P(None, ('px', 'py'))
- moved_adjoint: bfloat16 [640, 262144], P(None, ('px', 'py'))
Inputs may be any that keep to these rules, and one draw needn't show every extreme that they name: `block_inverse`: the inverse of the diagonal block shared by all faces. `raise_flag`: 1 marks an element raised in degree that moves to its new owner. `new_owner`: device index along px+py, px slowest; among one device's elements with raise_flag 1 at most 16 share one new owner, and in every draw one owner gets exactly 16 of them from every device.
All inputs are finite; a program needn't handle non-finite values.
Results may differ from a plain program's by a relative error of at most 0.0047.
Values may be sent and summed in bfloat16 or wider, within the bound.
A program may use at most 128 MiB of HBM per device.

v0:
```python
import functools

import jax
import jax.numpy as jnp
from jax import lax
from jax.experimental import pallas as pl
from jax.experimental.pallas import tpu as pltpu
from jax.sharding import PartitionSpec as P

NB = 80
NE = 320
NE_HI = 640
NF = 5 * NB
ROWS = 32
LANES = 128
CELLS = ROWS * LANES
CAP = 16
F32 = jnp.float32
BF16 = jnp.bfloat16
MESH = pl.DeviceIdType.MESH
NT = (((1,), (1,)), ((), ()))


def dot(a, b):
    return jnp.dot(a, b, preferred_element_type=F32)


def dot_nt(a, b):
    return lax.dot_general(a, b, NT, preferred_element_type=F32)


def block(i):
    return pl.ds(pl.multiple_of(i * LANES, LANES), LANES)


def pack_slots(slot_ref, picker, source_ref, out_ref, chunk):
    rows_iota = lax.broadcasted_iota(jnp.int32, (chunk, LANES), 0)

    def one_chunk(m, carry):
        for i in range(ROWS):
            row = slot_ref[pl.ds(i, 1), :] - m * chunk
            picker[:, i * LANES : (i + 1) * LANES] = jnp.where(row == rows_iota, 1.0, 0.0).astype(BF16)
        found = dot_nt(picker[...], source_ref[...])
        out_ref[pl.ds(pl.multiple_of(m * chunk, chunk), chunk), :] = found.astype(BF16)
        return carry

    lax.fori_loop(0, out_ref.shape[0] // chunk, one_chunk, 0)


def state_kernel(chunk, state_ref, owner_ref, flag_ref, sent_ref, flat_ref, slot_ref, wide, picker):
    step = 1024

    def widen(c, carry):
        at = pl.ds(pl.multiple_of(c * step, step), step)
        wide[at, :] = state_ref[at, :].astype(F32)
        return carry

    lax.fori_loop(0, NE * ROWS // step, widen, 0)
    for i in range(ROWS):
        flat_ref[:, i * LANES : (i + 1) * LANES] = wide[pl.ds(i, NE, stride=ROWS), :].astype(BF16)

    owner_iota = lax.broadcasted_iota(jnp.int32, (LANES, LANES), 0)
    first = lax.broadcasted_iota(jnp.int32, (LANES, 2 * LANES), 0)
    second = lax.broadcasted_iota(jnp.int32, (LANES, 2 * LANES), 1)
    tri = jnp.where(first < second, 1.0, 0.0).astype(BF16)
    before = jnp.zeros((LANES, LANES), F32)
    for i in range(ROWS):
        owner = owner_ref[i : i + 1, :]
        flag = flag_ref[i : i + 1, :]
        hot = jnp.where((owner == owner_iota) & (flag > 0), 1.0, 0.0)
        counts = dot(hot.astype(BF16), tri)
        rank = jnp.sum(hot * (counts[:, :LANES] + before), axis=0, keepdims=True).astype(jnp.int32)
        slot_ref[i : i + 1, :] = jnp.where(flag > 0, owner * CAP + rank, -1)
        before = before + counts[:, LANES:]
    pack_slots(slot_ref, picker, flat_ref, sent_ref, chunk)


def face_kernel(chunk, slot_ref, faces_ref, sent_ref, picker):
    pack_slots(slot_ref, picker, faces_ref, sent_ref, chunk)


def sweep_kernel(
    n_px,
    n_py,
    trace_ref,
    rhs_ref,
    scale_ref,
    coupling_ref,
    inverse_ref,
    final_ref,
    faces_ref,
    coupled,
    beside,
    partial,
    edge,
    outgoing,
    halo,
    send_sem,
    recv_sem,
):
    px, py = lax.axis_index("px"), lax.axis_index("py")
    down, up = lax.rem(px + 1, n_px), lax.rem(px + n_px - 1, n_px)
    right, left = lax.rem(py + 1, n_py), lax.rem(py + n_py - 1, n_py)
    targets = ((down, py), (up, py), (px, right), (px, left))
    barrier = pltpu.get_barrier_semaphore()
    for target in targets:
        pl.semaphore_signal(barrier, inc=1, device_id=target, device_id_type=MESH)
    lane = lax.broadcasted_iota(jnp.int32, (NB, LANES), 1)

    def copies(turn):
        return [
            pltpu.make_async_remote_copy(
                src_ref=outgoing.at[turn, d],
                dst_ref=halo.at[turn, d],
                send_sem=send_sem.at[turn, d],
                recv_sem=recv_sem.at[turn, d],
                device_id=targets[d],
                device_id_type=MESH,
            )
            for d in range(4)
        ]

    present = ((px > 0), (px < n_px - 1), (py > 0), (py < n_py - 1))

    def arrived(turn, d):
        return halo[turn, d].astype(F32) * present[d].astype(jnp.int32).astype(F32)

    def emit(values, g, k, into, base, stride, turn):
        i = g * 4 + k
        half = values.astype(BF16)
        if k < 3:
            into[base : base + NB, block(i + 1)] = half
        else:

            @pl.when(g < ROWS // 4 - 1)
            def _():
                into[base : base + NB, block(i + 1)] = half

            @pl.when(g == ROWS // 4 - 1)
            def _():
                outgoing[turn, 0] = half

        if k > 0:
            into[base + stride : base + stride + NB, block(i - 1)] = half
        else:

            @pl.when(g > 0)
            def _():
                into[base + stride : base + stride + NB, block(i - 1)] = half

            @pl.when(g == 0)
            def _():
                outgoing[turn, 1] = half

        to_right = jnp.where(lane >= 1, pltpu.roll(values, 1, 1), 0.0)
        to_left = jnp.where(lane < LANES - 1, pltpu.roll(values, LANES - 1, 1), 0.0)
        into[base + 2 * stride : base + 2 * stride + NB, block(i)] = to_right.astype(BF16)
        into[base + 3 * stride : base + 3 * stride + NB, block(i)] = to_left.astype(BF16)
        edge[0] = jnp.where(lane == i, pltpu.roll(values, i + 1, 1), edge[0])
        edge[1] = jnp.where(lane == i, pltpu.roll(values, i, 1), edge[1])

    def send_all(turn):
        outgoing[turn, 2] = edge[0].astype(BF16)
        outgoing[turn, 3] = edge[1].astype(BF16)
        for copy in copies(turn):
            copy.start()

    coupled[...] = jnp.zeros_like(coupled)
    beside[...] = jnp.zeros_like(beside)
    edge[...] = jnp.zeros_like(edge)
    for d in range(4):
        coupled[:, d * LANES : d * LANES + NB] = coupling_ref[d].astype(BF16)

    def load(g, carry):
        for k in range(4):
            emit(trace_ref[pl.ds(g * 4 + k, NB, stride=ROWS), :], g, k, beside, 0, LANES, 0)
        return carry

    lax.fori_loop(0, ROWS // 4, load, 0)
    pl.semaphore_wait(barrier, 4)
    send_all(0)

    for turn in range(2):

        def before_halo(g, carry):
            wide = pl.ds(pl.multiple_of(g * 4 * LANES, 4 * LANES), 4 * LANES)
            product = dot(coupled[...], beside[:, wide])
            for k in range(4):
                i = g * 4 + k
                partial[i] = rhs_ref[pl.ds(i, NB, stride=ROWS), :] - product[:, k * LANES : (k + 1) * LANES]
            return carry

        lax.fori_loop(0, ROWS // 4, before_halo, 0)
        for copy in copies(turn):
            copy.wait()
        from_halo = [
            dot(coupled[:, d * LANES : d * LANES + NB], arrived(turn, d).astype(BF16)) for d in range(4)
        ]
        partial[0] = partial[0] - from_halo[0]
        partial[ROWS - 1] = partial[ROWS - 1] - from_halo[1]

        def after_halo(g, carry):
            sums = []
            for k in range(4):
                i = g * 4 + k
                near = jnp.where(lane == 0, pltpu.roll(from_halo[2], lax.rem(LANES - i, LANES), 1), 0.0)
                far = jnp.where(lane == LANES - 1, pltpu.roll(from_halo[3], LANES - 1 - i, 1), 0.0)
                sums.append(partial[i] - near - far)
            joined = jnp.concatenate(sums, axis=1)
            high = joined.astype(BF16)
            low = (joined - high.astype(F32)).astype(BF16)
            product = dot(inverse_ref[...], jnp.concatenate([high, low, high], axis=0))
            for k in range(4):
                i = g * 4 + k
                values = product[:, k * LANES : (k + 1) * LANES] * scale_ref[pl.ds(i, 1), :]
                if turn == 0:
                    emit(values, g, k, beside, 0, LANES, 1)
                else:
                    final_ref[pl.ds(i, NB, stride=ROWS), :] = values
                    faces_ref[:NB, block(i)] = values.astype(BF16)
                    emit(values, g, k, faces_ref, NB, NB, 2)
            return carry

        lax.fori_loop(0, ROWS // 4, after_halo, 0)
        send_all(turn + 1)

    for copy in copies(2):
        copy.wait()
    faces_ref[NB : 2 * NB, :LANES] = arrived(2, 0).astype(BF16)
    faces_ref[2 * NB : 3 * NB, CELLS - LANES :] = arrived(2, 1).astype(BF16)
    from_left = arrived(2, 2)
    from_right = arrived(2, 3)

    def mend(g, carry):
        for k in range(4):
            i = g * 4 + k
            near = pltpu.roll(from_left, lax.rem(LANES - i, LANES), 1)
            far = pltpu.roll(from_right, LANES - 1 - i, 1)
            own = faces_ref[3 * NB : 4 * NB, block(i)].astype(F32)
            faces_ref[3 * NB : 4 * NB, block(i)] = jnp.where(lane == 0, near, own).astype(BF16)
            own = faces_ref[4 * NB :, block(i)].astype(F32)
            faces_ref[4 * NB :, block(i)] = jnp.where(lane == LANES - 1, far, own).astype(BF16)
        return carry

    lax.fori_loop(0, ROWS // 4, mend, 0)


def indicator_kernel(state_ref, faces_ref, self_ref, maps_ref, residual_ref, error_ref, out_ref):
    width = 4 * LANES
    for h in range(2):
        at = slice(h * width, (h + 1) * width)
        state = state_ref[:, at]
        recovered = dot(self_ref[...], state) + dot(maps_ref[...], faces_ref[:, at])
        weighted = dot(residual_ref[...], recovered.astype(BF16))
        residual = dot(error_ref[...], state)
        means = jnp.sum(jnp.abs(weighted * residual), axis=0, keepdims=True) * (1.0 / NE_HI)
        for k in range(4):
            out_ref[h * 4 + k : h * 4 + k + 1, :] = means[:, k * LANES : (k + 1) * LANES]


def raise_kernel(moved_ref, raise_ref, out_ref):
    out_ref[...] = dot_nt(raise_ref[...], moved_ref[...]).astype(BF16)


def owner_kernel(moved_ref, faces_ref, self_ref, maps_ref, out_ref):
    recovered = dot_nt(self_ref[...], moved_ref[...]) + dot_nt(maps_ref[...], faces_ref[...])
    out_ref[...] = recovered.astype(BF16)


def whole():
    return pl.BlockSpec(memory_space=pltpu.VMEM)


def fixed(shape):
    return pl.BlockSpec(shape, lambda i: (0, 0), pipeline_mode=pl.Buffered(1))


def cost(flops, bytes_accessed):
    return pl.CostEstimate(flops=flops, bytes_accessed=bytes_accessed, transcendentals=0)


def per_device(
    n_px,
    n_py,
    initial_trace,
    trace_rhs,
    face_scale,
    block_inverse,
    coupling,
    element_state,
    recover_self,
    recover_faces,
    residual_map,
    error_map,
    raise_map,
    raise_flag,
    new_owner,
):
    slots = n_px * n_py * CAP
    chunk = 512
    sent_state, flat_state, slot_index = pl.pallas_call(
        functools.partial(state_kernel, chunk),
        out_shape=(
            jax.ShapeDtypeStruct((slots, NE), BF16),
            jax.ShapeDtypeStruct((NE, CELLS), BF16),
            jax.ShapeDtypeStruct((ROWS, LANES), jnp.int32),
        ),
        in_specs=[whole()] * 3,
        out_specs=(whole(),) * 3,
        scratch_shapes=[pltpu.VMEM((NE * ROWS, LANES), F32), pltpu.VMEM((chunk, CELLS), BF16)],
        cost_estimate=cost(2 * slots * CELLS * NE, 8 << 20),
        name="state_pack",
    )(element_state.reshape(NE * ROWS, LANES), new_owner, raise_flag)
    moved_state = lax.all_to_all(sent_state, ("px", "py"), split_axis=0, concat_axis=0, tiled=True)

    inverse_high = block_inverse.astype(BF16)
    inverse_low = (block_inverse - inverse_high.astype(F32)).astype(BF16)
    inverse_split = jnp.concatenate([inverse_high, inverse_high, inverse_low], axis=1)
    final_trace, faces = pl.pallas_call(
        functools.partial(sweep_kernel, n_px, n_py),
        out_shape=(
            jax.ShapeDtypeStruct((NB * ROWS, LANES), F32),
            jax.ShapeDtypeStruct((NF, CELLS), BF16),
        ),
        in_specs=[whole()] * 5,
        out_specs=(whole(),) * 2,
        scratch_shapes=[
            pltpu.VMEM((NB, 4 * LANES), BF16),
            pltpu.VMEM((4 * LANES, CELLS), BF16),
            pltpu.VMEM((ROWS, NB, LANES), F32),
            pltpu.VMEM((2, NB, LANES), F32),
            pltpu.VMEM((3, 4, NB, LANES), BF16),
            pltpu.VMEM((3, 4, NB, LANES), BF16),
            pltpu.SemaphoreType.DMA((3, 4)),
            pltpu.SemaphoreType.DMA((3, 4)),
        ],
        compiler_params=pltpu.CompilerParams(collective_id=0, has_side_effects=True),
        cost_estimate=cost(15 << 30, 8 << 20),
        name="sweeps",
    )(
        initial_trace.reshape(NB * ROWS, LANES),
        trace_rhs.reshape(NB * ROWS, LANES),
        face_scale,
        coupling,
        inverse_split,
    )

    sent_faces = pl.pallas_call(
        functools.partial(face_kernel, chunk),
        out_shape=jax.ShapeDtypeStruct((slots, NF), BF16),
        in_specs=[whole()] * 2,
        out_specs=whole(),
        scratch_shapes=[pltpu.VMEM((chunk, CELLS), BF16)],
        cost_estimate=cost(2 * slots * CELLS * NF, 8 << 20),
        name="face_pack",
    )(slot_index, faces)
    moved_faces = lax.all_to_all(sent_faces, ("px", "py"), split_axis=0, concat_axis=0, tiled=True)

    face_maps = jnp.transpose(recover_faces, (1, 0, 2)).reshape(NE_HI, NF)
    width = 8 * LANES
    indicator = pl.pallas_call(
        indicator_kernel,
        out_shape=jax.ShapeDtypeStruct((ROWS, LANES), F32),
        grid=(CELLS // width,),
        in_specs=[
            pl.BlockSpec((NE, width), lambda i: (0, i)),
            pl.BlockSpec((NF, width), lambda i: (0, i)),
            fixed((NE_HI, NE)),
            fixed((NE_HI, NF)),
            fixed((NE_HI, NE_HI)),
            fixed((NE_HI, NE)),
        ],
        out_specs=pl.BlockSpec((8, LANES), lambda i: (i, 0)),
        cost_estimate=cost(2 * CELLS * NE_HI * (NE + NF + NE_HI + NE), 8 << 20),
        name="recover_indicator",
    )(flat_state, faces, recover_self, face_maps, residual_map, error_map)

    part = 512
    raised_state = pl.pallas_call(
        raise_kernel,
        out_shape=jax.ShapeDtypeStruct((NE_HI, slots), BF16),
        grid=(slots // part,),
        in_specs=[pl.BlockSpec((part, NE), lambda i: (i, 0)), fixed((NE_HI, NE))],
        out_specs=pl.BlockSpec((NE_HI, part), lambda i: (0, i)),
        cost_estimate=cost(2 * slots * NE_HI * NE, 5 << 20),
        name="owner_raise",
    )(moved_state, raise_map)
    moved_adjoint = pl.pallas_call(
        owner_kernel,
        out_shape=jax.ShapeDtypeStruct((NE_HI, slots), BF16),
        grid=(slots // part,),
        in_specs=[
            pl.BlockSpec((part, NE), lambda i: (i, 0)),
            pl.BlockSpec((part, NF), lambda i: (i, 0)),
            fixed((NE_HI, NE)),
            fixed((NE_HI, NF)),
        ],
        out_specs=pl.BlockSpec((NE_HI, part), lambda i: (0, i)),
        cost_estimate=cost(2 * slots * NE_HI * (NE + NF), 6 << 20),
        name="owner_recover",
    )(moved_state, moved_faces, recover_self, face_maps)
    return (final_trace.reshape(NB, ROWS, LANES), indicator, raised_state, moved_adjoint)


def solution(mesh):
    tiles = P(None, "px", "py")
    grid = P("px", "py")
    in_specs = (tiles, tiles, grid, P(), P(), tiles, P(), P(), P(), P(), P(), grid, grid)
    out_specs = (tiles, grid, P(None, ("px", "py")), P(None, ("px", "py")))
    return jax.shard_map(
        functools.partial(per_device, mesh.shape["px"], mesh.shape["py"]),
        mesh=mesh,
        in_specs=in_specs,
        out_specs=out_specs,
        check_vma=False,
    )
```

profile of v0, /device:TPU:1, one launch (start us, length us, event | category | flops | bytes accessed | tf_op | source)
XLA Modules:
  0.0 133.3 jit_solution(6502696758178120059)
XLA Ops:
  0.6 18.5 %state_pack.1 = (bf16[2048,320]{1,0:T(8,128)(2,1)}, bf16[320,4096]{1,0:T(8,128)(2,1)}, s32[32,128]{1,0:T(8,128)}) custom-call(bf16[10240,128]{1,0:T(8,128)(2,1)} %bitcast.17, s32[32,128]{1,0:T(8,128)} %owner_ref.1, s32[32,128]{1,0:T(8,128)} %flag_ref.1), custom_call_target="tpu_custom_call" | custom-call | flops 5368709120 | bytes 8388608 | tf_op jit(solution)/shard_map/state_pack/pallas_call | solution.py:301
  19.1 0.0 copy-start.6
  19.1 11.5 %all-to-all-start = ((bf16[128,16,320]{2,1,0:T(8,128)(2,1)}), bf16[128,16,320]{2,1,0:T(8,128)(2,1)S(1)}, u32[]{:S(2)}, u32[]{:S(2)}) async-start(bf16[128,16,320]{2,1,0:T(8,128)(2,1)} %bitcast.14), calls=%async_computation | async-start | bytes 3145728 | tf_op jit(solution)/shard_map/all_to_all | solution.py:314
  30.6 0.0 copy-done.6
  30.7 0.7 pad_maximum_fusion.inverse_ref
  31.4 42.9 %sweeps.1 = (f32[2560,128]{1,0:T(8,128)}, bf16[400,4096]{1,0:T(8,128)(2,1)}) custom-call(f32[2560,128]{1,0:T(8,128)} %bitcast.18, f32[2560,128]{1,0:T(8,128)} %bitcast.19, f32[32,128]{1,0:T(8,128)} %scale_ref.1, f32[4,80,80]{2,1,0:T(8,128)} %coupling_ref.1, bf16[80,240]{1,0:T(8,128)(2,1)} %pad_maximum_fusion.inverse_ref), custom_call_target="tpu_custom_call" | custom-call | flops 16106127360 | bytes 8388608 | tf_op jit(solution)/shard_map/sweeps/pallas_call | solution.py:319
  74.2 12.7 %face_pack.1 = bf16[2048,400]{1,0:T(8,128)(2,1)} custom-call(s32[32,128]{1,0:T(8,128)} %get-tuple-element.13.slot_ref, bf16[400,4096]{1,0:T(8,128)(2,1)} %get-tuple-element.11.faces_ref), custom_call_target="tpu_custom_call" | custom-call | flops 6710886400 | bytes 8388608 | tf_op jit(solution)/shard_map/face_pack/pallas_call | solution.py:348
  87.0 0.0 all-to-all-done
  87.0 0.0 copy-start
  87.0 0.0 copy-start.3
  87.0 0.0 copy-start.2
  87.0 0.0 copy-start.4
  87.0 1.2 copy-done
  88.2 8.2 %all-to-all-start.1 = ((bf16[128,16,400]{2,1,0:T(8,128)(2,1)}), bf16[128,16,400]{2,1,0:T(8,128)(2,1)}, u32[]{:S(2)}, u32[]{:S(2)}) async-start(bf16[128,16,400]{2,1,0:T(8,128)(2,1)} %bitcast.13), calls=%async_computation.1 | async-start | bytes 4194304 | tf_op jit(solution)/shard_map/all_to_all | solution.py:357
  96.4 0.0 copy-start.5
  96.4 0.0 copy-done.3
  96.4 1.0 copy.22.self_ref
  97.4 0.0 copy-done.2
  97.4 1.1 copy.23.maps_ref
  98.5 0.0 copy-done.4
  98.5 1.0 copy.24.error_ref
  99.5 0.0 copy-done.5
  99.5 1.0 copy.25.raise_ref
  100.5 15.9 %recover_indicator.1 = f32[32,128]{1,0:T(8,128)} custom-call(bf16[320,4096]{1,0:T(8,128)(2,1)} %get-tuple-element.10.state_ref, bf16[400,4096]{1,0:T(8,128)(2,1)} %get-tuple-element.11.faces_ref, bf16[640,320]{1,0:T(8,128)(2,1)} %copy.22.self_ref, bf16[640,400]{1,0:T(8,128)(2,1)} %copy.23.maps_ref, bf16[640,640]{1,0:T(8,128)(2,1)} %residual_ref.1, ...), custom_call_target="tpu_custom_call" | custom-call | flops 8808038400 | bytes 8388608 | tf_op jit(solution)/shard_map/recover_indicator/pallas_call | solution.py:361
  116.5 4.9 %owner_raise.1 = bf16[640,2048]{1,0:T(8,128)(2,1)} custom-call(bf16[2048,320]{1,0:T(8,128)(2,1)} %bitcast.11, bf16[640,320]{1,0:T(8,128)(2,1)} %copy.25.raise_ref), custom_call_target="tpu_custom_call" | custom-call | flops 838860800 | bytes 5242880 | tf_op jit(solution)/shard_map/owner_raise/pallas_call | solution.py:379
  121.4 4.3 %all-to-all-done.1 = bf16[128,16,400]{2,1,0:T(8,128)(2,1)} async-done(((bf16[128,16,400]{2,1,0:T(8,128)(2,1)}), bf16[128,16,400]{2,1,0:T(8,128)(2,1)}, u32[]{:S(2)}, u32[]{:S(2)}) %all-to-all-start.1) | async-done | bytes 1638432 | tf_op jit(solution)/shard_map/all_to_all | solution.py:357
  125.7 0.0 copy-start.1
  125.7 6.6 %owner_recover.1 = bf16[640,2048]{1,0:T(8,128)(2,1)} custom-call(bf16[2048,320]{1,0:T(8,128)(2,1)} %bitcast.12, bf16[2048,400]{1,0:T(8,128)(2,1)} %bitcast.9.faces_ref, bf16[640,320]{1,0:T(8,128)(2,1)} %copy.22.self_ref, bf16[640,400]{1,0:T(8,128)(2,1)} %copy.23.maps_ref), custom_call_target="tpu_custom_call" | custom-call | flops 1887436800 | bytes 6291456 | tf_op jit(solution)/shard_map/owner_recover/pallas_call | solution.py:388
  132.3 0.0 copy-done.1
  132.3 1.1 copy.29
  (1 shorter events, 0.0 us)
Async XLA Ops:
  19.1 11.5 %copy-start.6 = (f32[80,80]{1,0:T(8,128)S(1)}, f32[80,80]{1,0:T(8,128)}, u32[]{:S(2)}) copy-start(f32[80,80]{1,0:T(8,128)} %param.16) | copy-start | bytes 76804
  19.1 67.9 %all-to-all-start = ((bf16[128,16,320]{2,1,0:T(8,128)(2,1)}), bf16[128,16,320]{2,1,0:T(8,128)(2,1)S(1)}, u32[]{:S(2)}, u32[]{:S(2)}) async-start(bf16[128,16,320]{2,1,0:T(8,128)(2,1)} %bitcast.14), calls=%async_computation | async-start | bytes 3145728 | tf_op jit(solution)/shard_map/all_to_all | solution.py:314
  87.0 1.2 copy-start
  87.0 9.4 %copy-start.3 = (bf16[640,320]{0,1:T(8,128)(2,1)S(1)}, bf16[640,320]{0,1:T(8,128)(2,1)}, u32[]{:S(2)}) copy-start(bf16[640,320]{0,1:T(8,128)(2,1)} %param.19) | copy-start | bytes 1228804
  87.0 10.4 %copy-start.2 = (bf16[5,640,80]{1,2,0:T(8,128)(2,1)S(1)}, bf16[5,640,80]{1,2,0:T(8,128)(2,1)}, u32[]{:S(2)}) copy-start(bf16[5,640,80]{1,2,0:T(8,128)(2,1)} %param.20) | copy-start | bytes 1536004
  87.0 11.5 %copy-start.4 = (bf16[640,320]{0,1:T(8,128)(2,1)S(1)}, bf16[640,320]{0,1:T(8,128)(2,1)}, u32[]{:S(2)}) copy-start(bf16[640,320]{0,1:T(8,128)(2,1)} %param.22) | copy-start | bytes 1228804
  88.2 37.4 %all-to-all-start.1 = ((bf16[128,16,400]{2,1,0:T(8,128)(2,1)}), bf16[128,16,400]{2,1,0:T(8,128)(2,1)}, u32[]{:S(2)}, u32[]{:S(2)}) async-start(bf16[128,16,400]{2,1,0:T(8,128)(2,1)} %bitcast.13), calls=%async_computation.1 | async-start | bytes 4194304 | tf_op jit(solution)/shard_map/all_to_all | solution.py:357
  96.4 3.1 %copy-start.5 = (bf16[640,320]{0,1:T(8,128)(2,1)S(1)}, bf16[640,320]{0,1:T(8,128)(2,1)}, u32[]{:S(2)}) copy-start(bf16[640,320]{0,1:T(8,128)(2,1)} %param.23) | copy-start | bytes 1228804
  125.7 6.6 %copy-start.1 = (f32[2560,128]{1,0:T(8,128)S(1)}, f32[2560,128]{1,0:T(8,128)}, u32[]{:S(2)}) copy-start(f32[2560,128]{1,0:T(8,128)} %get-tuple-element.9) | copy-start | bytes 3932164
where the time goes:
time: 134 us; the launch traced here: 133 us
  Pallas kernels  102 us (76%)
  starting transfers between devices  19.7 us (15%)
  local copies, waits for them, and re-layouts  6.4 us (5%)
  waiting for transfers between devices  4.29 us (3%)
    pallas_call x1, Pallas kernels, per_device(): pl.pallas_call(functools.partial(sweep_kernel, n_px, n_py), out_shape=(ja...  42.9 us
    pallas_call x1, Pallas kernels, per_device(): pl.pallas_call(functools.partial(state_kernel, chunk), out_shape=(jax.Sha...  18.5 us
    pallas_call x1, Pallas kernels, per_device(): pl.pallas_call(indicator_kernel, out_shape=jax.ShapeDtypeStruct((ROWS, LA...  15.9 us
    pallas_call x1, Pallas kernels, per_device(): pl.pallas_call(functools.partial(face_kernel, chunk), out_shape=jax.Shape...  12.7 us
    all_to_all x1, starting transfers between devices, per_device(): lax.all_to_all(sent_state, ('px', 'py'), split_axis=0, concat_axis=0, til...  11.5 us
    all_to_all x1, starting transfers between devices, per_device(): lax.all_to_all(sent_faces, ('px', 'py'), split_axis=0, concat_axis=0, til...  8.17 us
    pallas_call x1, Pallas kernels, per_device(): pl.pallas_call(owner_kernel, out_shape=jax.ShapeDtypeStruct((NE_HI, slots...  6.6 us
    unnamed x18, local copies, waits for them, and re-layouts  5.31 us
  transfers between devices with their start and end apart: 2, of which 1 were waited for; matrix products, arithmetic and copies ran while one was open for 4% of the time, Pallas kernels for 57%

commit v1 on v0

v1 whole, which is shorter than its diff:
```python
import functools

import jax
import jax.numpy as jnp
from jax import lax
from jax.experimental import pallas as pl
from jax.experimental.pallas import tpu as pltpu
from jax.sharding import PartitionSpec as P

NB = 80
NE = 320
NE_HI = 640
NF = 5 * NB
EARLY = 256
REST = NE - EARLY
LATE = 512
GROUP = 512
ROWS = 32
LANES = 128
CELLS = ROWS * LANES
CAP = 16
F32 = jnp.float32
BF16 = jnp.bfloat16
MESH = pl.DeviceIdType.MESH
NT = (((1,), (1,)), ((), ()))


def dot(a, b):
    return jnp.dot(a, b, preferred_element_type=F32)


def dot_nt(a, b):
    return lax.dot_general(a, b, NT, preferred_element_type=F32)


def block(i):
    return pl.ds(pl.multiple_of(i * LANES, LANES), LANES)


def turned(matrix, count):
    eye_row = lax.broadcasted_iota(jnp.int32, (LANES, LANES), 0)
    eye_col = lax.broadcasted_iota(jnp.int32, (LANES, LANES), 1)
    eye = jnp.where(eye_row == eye_col, 1.0, 0.0).astype(BF16)
    parts = [dot_nt(eye, matrix[:, c * LANES : (c + 1) * LANES]) for c in range(count // LANES)]
    return jnp.concatenate(parts, axis=0).astype(BF16)


def main_kernel(
    n_px,
    n_py,
    state_ref,
    owner_ref,
    flag_ref,
    trace_ref,
    rhs_ref,
    scale_ref,
    coupling_ref,
    inverse_ref,
    self_ref,
    maps_ref,
    residual_ref,
    error_ref,
    raise_ref,
    final_ref,
    indicator_ref,
    moved_early,
    moved_late,
    weights_ref,
    wide,
    early,
    late,
    slots,
    picker,
    sent_early,
    sent_late,
    late_maps,
    coupled,
    beside,
    partial,
    outgoing,
    halo,
    send_sem,
    recv_sem,
    early_send,
    early_recv,
    late_send,
    late_recv,
    self_sem,
):
    px, py = lax.axis_index("px"), lax.axis_index("py")
    devices = n_px * n_py
    me = px * n_py + py
    down, up = lax.rem(px + 1, n_px), lax.rem(px + n_px - 1, n_px)
    right, left = lax.rem(py + 1, n_py), lax.rem(py + n_py - 1, n_py)
    targets = ((down, py), (up, py), (px, right), (px, left))
    barrier = pltpu.get_barrier_semaphore()

    def place(device):
        return (lax.div(device, n_py), lax.rem(device, n_py))

    def greet(k, carry):
        pl.semaphore_signal(
            barrier, inc=1, device_id=place(lax.rem(me + k, devices)), device_id_type=MESH
        )
        return carry

    lax.fori_loop(1, devices, greet, 0)
    lane = lax.broadcasted_iota(jnp.int32, (NB, LANES), 1)

    def copies(turn):
        return [
            pltpu.make_async_remote_copy(
                src_ref=outgoing.at[turn, d],
                dst_ref=halo.at[turn, d],
                send_sem=send_sem.at[turn, d],
                recv_sem=recv_sem.at[turn, d],
                device_id=targets[d],
                device_id_type=MESH,
            )
            for d in range(4)
        ]

    present = ((px > 0), (px < n_px - 1), (py > 0), (py < n_py - 1))

    def arrived(turn, d):
        return halo[turn, d].astype(F32) * present[d].astype(jnp.int32).astype(F32)

    def emit(values, i, into, base, stride, turn, edges):
        half = values.astype(BF16)
        if i < ROWS - 1:
            into[base : base + NB, (i + 1) * LANES : (i + 2) * LANES] = half
        else:
            outgoing[turn, 0] = half
        if i > 0:
            into[base + stride : base + stride + NB, (i - 1) * LANES : i * LANES] = half
        else:
            outgoing[turn, 1] = half
        at = slice(i * LANES, (i + 1) * LANES)
        to_right = pltpu.roll(values, 1, 1)
        to_left = pltpu.roll(values, LANES - 1, 1)
        into[base + 2 * stride : base + 2 * stride + NB, at] = jnp.where(lane >= 1, to_right, 0.0).astype(BF16)
        into[base + 3 * stride : base + 3 * stride + NB, at] = jnp.where(
            lane < LANES - 1, to_left, 0.0
        ).astype(BF16)
        last = pltpu.roll(values, i + 1, 1)
        first = pltpu.roll(values, i, 1) if i else values
        return jnp.where(lane == i, last, edges[0]), jnp.where(lane == i, first, edges[1])

    def send_all(turn, edges):
        outgoing[turn, 2] = edges[0].astype(BF16)
        outgoing[turn, 3] = edges[1].astype(BF16)
        for copy in copies(turn):
            copy.start()

    no_edges = (jnp.zeros((NB, LANES), F32),) * 2

    def send_blocks(source, target_ref, sent_sem, got_sem):
        def one(k, carry):
            to = lax.rem(me + k, devices)
            pltpu.make_async_remote_copy(
                src_ref=source.at[to],
                dst_ref=target_ref.at[me],
                send_sem=sent_sem,
                recv_sem=got_sem,
                device_id=place(to),
                device_id_type=MESH,
            ).start()
            return carry

        lax.fori_loop(1, devices, one, 0)

    def wait_blocks(source, target_ref, sent_sem, got_sem):
        all_but_one = pl.ds(0, devices - 1)
        everything = pltpu.make_async_remote_copy(
            src_ref=source.at[all_but_one],
            dst_ref=target_ref.at[all_but_one],
            send_sem=sent_sem,
            recv_sem=got_sem,
            device_id=targets[0],
            device_id_type=MESH,
        )
        everything.wait_recv()
        everything.wait_send()

    def pack(source, out, first, last):
        def one(m, carry):
            at = pl.ds(pl.multiple_of(m * GROUP, GROUP), GROUP)
            found = dot_nt(picker[at, :], source[...]).astype(BF16)
            blocks = pl.ds(pl.multiple_of(m * (GROUP // CAP), GROUP // CAP), GROUP // CAP)
            out[blocks, :, :] = found.reshape(GROUP // CAP, CAP, source.shape[0])
            return carry

        lax.fori_loop(first, last, one, 0)

    def state_layout():
        step = 1024
        for c in range(NE * ROWS // step):
            at = slice(c * step, (c + 1) * step)
            wide[at, :] = state_ref[at, :].astype(F32)
        for i in range(ROWS):
            at = slice(i * LANES, (i + 1) * LANES)
            early[:, at] = wide[pl.ds(i, EARLY, stride=ROWS), :].astype(BF16)
            late[:REST, at] = wide[pl.ds(EARLY * ROWS + i, REST, stride=ROWS), :].astype(BF16)
        late[REST + NF :, :] = jnp.zeros((LATE - REST - NF, CELLS), BF16)

    def number_slots():
        owner_iota = lax.broadcasted_iota(jnp.int32, (LANES, LANES), 0)
        first = lax.broadcasted_iota(jnp.int32, (LANES, 2 * LANES), 0)
        second = lax.broadcasted_iota(jnp.int32, (LANES, 2 * LANES), 1)
        tri = jnp.where(first < second, 1.0, 0.0).astype(BF16)
        before = jnp.zeros((LANES, LANES), F32)
        for i in range(ROWS):
            owner = owner_ref[i : i + 1, :]
            flag = flag_ref[i : i + 1, :]
            hot = jnp.where((owner == owner_iota) & (flag > 0), 1.0, 0.0)
            counts = dot(hot.astype(BF16), tri)
            rank = jnp.sum(hot * (counts[:, :LANES] + before), axis=0, keepdims=True).astype(jnp.int32)
            slots[i : i + 1, :] = jnp.where(flag > 0, owner * CAP + rank, -1)
            before = before + counts[:, LANES:]

    def build_picker():
        size = 256
        rows_iota = lax.broadcasted_iota(jnp.int32, (size, LANES), 0).astype(F32).astype(BF16)
        one, zero = jnp.ones((), BF16), jnp.zeros((), BF16)

        def fill(m, carry):
            for i in range(ROWS):
                row = slots[i : i + 1, :] - m * size
                row = jnp.where((row >= 0) & (row < size), row, -1).astype(F32).astype(BF16)
                hit = jnp.where(row == rows_iota, one, zero)
                picker[pl.ds(pl.multiple_of(m * size, size), size), i * LANES : (i + 1) * LANES] = hit
            return carry

        lax.fori_loop(0, picker.shape[0] // size, fill, 0)

    def between(turn):
        if turn == 0:
            build_picker()
            pack(early, sent_early, 0, picker.shape[0] // GROUP)
        else:
            send_blocks(sent_early, moved_early, early_send, early_recv)

    coupled[...] = jnp.zeros_like(coupled)
    for d in range(4):
        coupled[:, d * LANES : d * LANES + NB] = coupling_ref[d].astype(BF16)
        beside[d * LANES + NB : (d + 1) * LANES, :] = jnp.zeros((LANES - NB, CELLS), BF16)
    beside[:NB, :LANES] = jnp.zeros((NB, LANES), BF16)
    beside[LANES : LANES + NB, CELLS - LANES :] = jnp.zeros((NB, LANES), BF16)

    state_layout()
    number_slots()
    edges = no_edges
    for i in range(ROWS):
        edges = emit(trace_ref[pl.ds(i, NB, stride=ROWS), :], i, beside, 0, LANES, 0, edges)
    pl.semaphore_wait(barrier, devices - 1)
    send_all(0, edges)
    for turn in range(2):
        between(turn)
        for g in range(ROWS // 4):
            product = dot(coupled[...], beside[:, g * 4 * LANES : (g + 1) * 4 * LANES])
            for k in range(4):
                i = g * 4 + k
                partial[i] = rhs_ref[pl.ds(i, NB, stride=ROWS), :] - product[:, k * LANES : (k + 1) * LANES]
        for copy in copies(turn):
            copy.wait()
        from_halo = [
            dot(coupled[:, d * LANES : d * LANES + NB], arrived(turn, d).astype(BF16)) for d in range(4)
        ]
        edges = no_edges
        for g in range(ROWS // 4):
            sums = []
            for k in range(4):
                i = g * 4 + k
                near = pltpu.roll(from_halo[2], LANES - i, 1) if i else from_halo[2]
                far = pltpu.roll(from_halo[3], LANES - 1 - i, 1)
                total = partial[i] - jnp.where(lane == 0, near, 0.0) - jnp.where(lane == LANES - 1, far, 0.0)
                if i == 0:
                    total = total - from_halo[0]
                if i == ROWS - 1:
                    total = total - from_halo[1]
                sums.append(total)
            joined = jnp.concatenate(sums, axis=1)
            high = joined.astype(BF16)
            low = (joined - high.astype(F32)).astype(BF16)
            product = dot(inverse_ref[...], jnp.concatenate([high, low, high], axis=0))
            for k in range(4):
                i = g * 4 + k
                values = product[:, k * LANES : (k + 1) * LANES] * scale_ref[i : i + 1, :]
                if turn == 0:
                    edges = emit(values, i, beside, 0, LANES, 1, edges)
                else:
                    final_ref[pl.ds(i, NB, stride=ROWS), :] = values
                    late[REST : REST + NB, i * LANES : (i + 1) * LANES] = values.astype(BF16)
                    edges = emit(values, i, late, REST + NB, NB, 2, edges)
        send_all(turn + 1, edges)


    late_maps[:REST, :] = self_ref[EARLY:, :]
    late_maps[REST : REST + NF, :] = maps_ref[...]
    late_maps[REST + NF :, :] = jnp.zeros((LATE - REST - NF, NE_HI), BF16)
    no_rest = jnp.zeros((LANES - REST, NE_HI), BF16)
    weigh_early = dot_nt(residual_ref[...], self_ref[:EARLY, :]).astype(BF16)
    weigh_late = dot_nt(residual_ref[...], late_maps[...]).astype(BF16)
    error_early = turned(error_ref[:EARLY, :], NE_HI)
    error_late = turned(jnp.concatenate([error_ref[EARLY:, :], no_rest], axis=0), NE_HI)
    weights_ref[:, :EARLY] = weigh_early
    weights_ref[:, EARLY : EARLY + LATE] = weigh_late
    weights_ref[:, EARLY + LATE : 2 * EARLY + LATE] = error_early
    weights_ref[:, 2 * EARLY + LATE :] = error_late
    for copy in copies(2):
        copy.wait()
    late[REST + NB : REST + 2 * NB, :LANES] = arrived(2, 0).astype(BF16)
    late[REST + 2 * NB : REST + 3 * NB, CELLS - LANES :] = arrived(2, 1).astype(BF16)
    from_left = arrived(2, 2)
    from_right = arrived(2, 3)
    for i in range(ROWS):
        at = slice(i * LANES, (i + 1) * LANES)
        near = pltpu.roll(from_left, LANES - i, 1) if i else from_left
        far = pltpu.roll(from_right, LANES - 1 - i, 1) if i < LANES - 1 else from_right
        own = late[REST + 3 * NB : REST + 4 * NB, at].astype(F32)
        late[REST + 3 * NB : REST + 4 * NB, at] = jnp.where(lane == 0, near, own).astype(BF16)
        own = late[REST + 4 * NB : REST + 5 * NB, at].astype(F32)
        late[REST + 4 * NB : REST + 5 * NB, at] = jnp.where(lane == LANES - 1, far, own).astype(BF16)
    pack(late, sent_late, 0, picker.shape[0] // GROUP)
    send_blocks(sent_late, moved_late, late_send, late_recv)
    own_early = pltpu.make_async_copy(sent_early.at[me], moved_early.at[me], self_sem.at[0])
    own_late = pltpu.make_async_copy(sent_late.at[me], moved_late.at[me], self_sem.at[1])
    own_early.start()
    own_late.start()

    width = 4 * LANES

    def measure(h, carry):
        at = pl.ds(pl.multiple_of(h * width, width), width)
        first, second = early[:, at], late[:, at]
        weighted = dot(weights_ref[:, :EARLY], first) + dot(weights_ref[:, EARLY : EARLY + LATE], second)
        residual = dot(weights_ref[:, EARLY + LATE : 2 * EARLY + LATE], first) + dot(
            weights_ref[:, 2 * EARLY + LATE :], second[:LANES, :]
        )
        means = jnp.sum(jnp.abs(weighted * residual), axis=0, keepdims=True) * (1.0 / NE_HI)
        for k in range(4):
            indicator_ref[pl.ds(h * 4 + k, 1), :] = means[:, k * LANES : (k + 1) * LANES]
        return carry

    lax.fori_loop(0, CELLS // width, measure, 0)

    weights_ref[:, :EARLY] = turned(self_ref[:EARLY, :], NE_HI)
    weights_ref[:, EARLY : EARLY + LATE] = turned(late_maps[...], NE_HI)
    weights_ref[:, EARLY + LATE : 2 * EARLY + LATE] = turned(raise_ref[:EARLY, :], NE_HI)
    weights_ref[:, 2 * EARLY + LATE :] = turned(
        jnp.concatenate([raise_ref[EARLY:, :], no_rest], axis=0), NE_HI
    )
    own_early.wait()
    own_late.wait()
    wait_blocks(sent_early, moved_early, early_send, early_recv)
    wait_blocks(sent_late, moved_late, late_send, late_recv)


def owner_kernel(early_ref, late_ref, weights_ref, raised_ref, adjoint_ref):
    part = raised_ref.shape[1]
    early = early_ref[...].reshape(part, EARLY)
    late = late_ref[...].reshape(part, LATE)
    raised = dot_nt(weights_ref[:, EARLY + LATE : 2 * EARLY + LATE], early) + dot_nt(
        weights_ref[:, 2 * EARLY + LATE :], late[:, :LANES]
    )
    raised_ref[...] = raised.astype(BF16)
    recovered = dot_nt(weights_ref[:, :EARLY], early) + dot_nt(weights_ref[:, EARLY : EARLY + LATE], late)
    adjoint_ref[...] = recovered.astype(BF16)


def whole():
    return pl.BlockSpec(memory_space=pltpu.VMEM)


def per_device(
    n_px,
    n_py,
    initial_trace,
    trace_rhs,
    face_scale,
    block_inverse,
    coupling,
    element_state,
    recover_self,
    recover_faces,
    residual_map,
    error_map,
    raise_map,
    raise_flag,
    new_owner,
):
    devices = n_px * n_py
    slots = devices * CAP
    inverse_high = block_inverse.astype(BF16)
    inverse_low = (block_inverse - inverse_high.astype(F32)).astype(BF16)
    inverse_split = jnp.concatenate([inverse_high, inverse_high, inverse_low], axis=1)
    final_trace, indicator, moved_early, moved_late, weights = pl.pallas_call(
        functools.partial(main_kernel, n_px, n_py),
        out_shape=(
            jax.ShapeDtypeStruct((NB * ROWS, LANES), F32),
            jax.ShapeDtypeStruct((ROWS, LANES), F32),
            jax.ShapeDtypeStruct((devices, CAP, EARLY), BF16),
            jax.ShapeDtypeStruct((devices, CAP, LATE), BF16),
            jax.ShapeDtypeStruct((NE_HI, 2 * EARLY + LATE + LANES), BF16),
        ),
        in_specs=[whole()] * 13,
        out_specs=(whole(),) * 5,
        scratch_shapes=[
            pltpu.VMEM((NE * ROWS, LANES), F32),
            pltpu.VMEM((EARLY, CELLS), BF16),
            pltpu.VMEM((LATE, CELLS), BF16),
            pltpu.VMEM((ROWS, LANES), jnp.int32),
            pltpu.VMEM((slots, CELLS), BF16),
            pltpu.VMEM((devices, CAP, EARLY), BF16),
            pltpu.VMEM((devices, CAP, LATE), BF16),
            pltpu.VMEM((LATE, NE_HI), BF16),
            pltpu.VMEM((NB, 4 * LANES), BF16),
            pltpu.VMEM((4 * LANES, CELLS), BF16),
            pltpu.VMEM((ROWS, NB, LANES), F32),
            pltpu.VMEM((3, 4, NB, LANES), BF16),
            pltpu.VMEM((3, 4, NB, LANES), BF16),
            pltpu.SemaphoreType.DMA((3, 4)),
            pltpu.SemaphoreType.DMA((3, 4)),
            pltpu.SemaphoreType.DMA,
            pltpu.SemaphoreType.DMA,
            pltpu.SemaphoreType.DMA,
            pltpu.SemaphoreType.DMA,
            pltpu.SemaphoreType.DMA((2,)),
        ],
        compiler_params=pltpu.CompilerParams(
            collective_id=0, has_side_effects=True, vmem_limit_bytes=64000 * 1024
        ),
        name="main",
    )(
        element_state.reshape(NE * ROWS, LANES),
        new_owner,
        raise_flag,
        initial_trace.reshape(NB * ROWS, LANES),
        trace_rhs.reshape(NB * ROWS, LANES),
        face_scale,
        coupling,
        inverse_split,
        recover_self.T,
        jnp.transpose(recover_faces, (0, 2, 1)).reshape(NF, NE_HI),
        residual_map,
        error_map.T,
        raise_map.T,
    )

    part = 32
    raised_state, moved_adjoint = pl.pallas_call(
        owner_kernel,
        out_shape=(jax.ShapeDtypeStruct((NE_HI, slots), BF16),) * 2,
        grid=(devices // part,),
        in_specs=[
            pl.BlockSpec((part, CAP, EARLY), lambda i: (i, 0, 0)),
            pl.BlockSpec((part, CAP, LATE), lambda i: (i, 0, 0)),
            pl.BlockSpec(weights.shape, lambda i: (0, 0), pipeline_mode=pl.Buffered(1)),
        ],
        out_specs=(pl.BlockSpec((NE_HI, part * CAP), lambda i: (0, i)),) * 2,
        name="owner",
    )(moved_early, moved_late, weights)
    return (final_trace.reshape(NB, ROWS, LANES), indicator, raised_state, moved_adjoint)


def solution(mesh):
    tiles = P(None, "px", "py")
    grid = P("px", "py")
    in_specs = (tiles, tiles, grid, P(), P(), tiles, P(), P(), P(), P(), P(), grid, grid)
    out_specs = (tiles, grid, P(None, ("px", "py")), P(None, ("px", "py")))
    return jax.shard_map(
        functools.partial(per_device, mesh.shape["px"], mesh.shape["py"]),
        mesh=mesh,
        in_specs=in_specs,
        out_specs=out_specs,
        check_vma=False,
    )
```

time: 134 us -> 100 us (0.75)
  starting transfers between devices: 19.7 us -> 0 us
  Pallas kernels: 102 us -> 95.3 us
  local copies, waits for them, and re-layouts: 6.4 us -> 1.67 us
  waiting for transfers between devices: 4.29 us -> 0 us
    all_to_all x2 -> x0, starting transfers between devices: 19.7 us -> none  [the longest x1 11.5 us: per_device(): lax.all_to_all(sent_state, ('px', 'py'), split_axis=0, concat_axis=0, til...]
    pallas_call x6 -> x2, Pallas kernels: 102 us -> 95.3 us  [the longest x1 88.3 us: per_device(): pl.pallas_call(functools.partial(main_kernel, n_px, n_py), out_shape=(jax...]
    all_to_all x2 -> x0, waiting for transfers between devices: 4.29 us -> none  [the longest x1 4.29 us: per_device(): lax.all_to_all(sent_faces, ('px', 'py'), split_axis=0, concat_axis=0, til...]
    unnamed x18 -> x6, local copies, waits for them, and re-layouts: 5.31 us -> 1.67 us
  transfers between devices with their start and end apart: 2 -> 0, of which waited for: 1 -> 0; matrix products, arithmetic and copies ran while one was open for 4% -> 0% of each run, Pallas kernels for 57% -> 0%
where the time goes in v1:
time: 100 us; the launch traced here: 99.2 us
  Pallas kernels  95.3 us (95%)
  local copies, waits for them, and re-layouts  1.67 us (2%)
  other arithmetic  1.57 us (2%)
    pallas_call x1, Pallas kernels, per_device(): pl.pallas_call(functools.partial(main_kernel, n_px, n_py), out_shape=(jax...  88.3 us
    pallas_call x1, Pallas kernels, per_device(): pl.pallas_call(owner_kernel, out_shape=(jax.ShapeDtypeStruct((NE_HI, slot...  7.05 us

profile of v1, /device:TPU:1, one launch (start us, length us, event | category | flops | bytes accessed | tf_op | source)
XLA Modules:
  0.0 99.2 jit_solution(6774345582240809529)
XLA Ops:
  0.6 0.9 subtract_convert_fusion
  1.5 0.7 pad_maximum_fusion.inverse_ref
  2.2 88.3 %main.1 = (f32[2560,128]{1,0:T(8,128)}, f32[32,128]{1,0:T(8,128)}, bf16[128,16,256]{2,1,0:T(8,128)(2,1)}, bf16[128,16,512]{2,1,0:T(8,128)(2,1)}, bf16[640,1152]{1,0:T(8,128)(2,1)}) custom-call(bf16[10240,128]{1,0:T(8,128)(2,1)} %bitcast.10, s32[32,128]{1,0:T(8,128)} %owner_ref.1, s32[32,128]{1,0:T(8,128)} %flag_ref.1, f32[2560,128]{1,0:T(8,128)} %bitcast.11, ...), custom_call_target="tpu_custom_call" | custom-call | tf_op jit(solution)/shard_map/main/pallas_call | solution.py:397
  90.5 0.0 copy-start
  90.5 7.1 %owner.1 = (bf16[640,2048]{1,0:T(8,128)(2,1)}, bf16[640,2048]{1,0:T(8,128)(2,1)}) custom-call(bf16[128,16,256]{2,1,0:T(8,128)(2,1)} %get-tuple-element.13.early_ref, bf16[128,16,512]{2,1,0:T(8,128)(2,1)} %get-tuple-element.14.late_ref, bf16[640,1152]{1,0:T(8,128)(2,1)} %get-tuple-element.15.weights_ref), custom_call_target="tpu_custom_call" | custom-call | tf_op jit(solution)/shard_map/owner/pallas_call | solution.py:451
  97.5 0.0 copy-start.1
  97.5 0.0 copy-done
  97.6 1.1 %copy.19 = f32[80,32,128]{2,1,0:T(8,128)} copy(f32[80,32,128]{2,1,0:T(8,128)S(1)} %bitcast.13) | data formatting | bytes 2621440
  98.6 0.0 copy-done.1
  98.6 0.6 copy.20
Async XLA Ops:
  90.5 7.1 %copy-start = (f32[2560,128]{1,0:T(8,128)S(1)}, f32[2560,128]{1,0:T(8,128)}, u32[]{:S(2)}) copy-start(f32[2560,128]{1,0:T(8,128)} %get-tuple-element.11) | copy-start | bytes 3932164
  97.5 1.1 %copy-start.1 = (f32[32,128]{1,0:T(8,128)S(1)}, f32[32,128]{1,0:T(8,128)}, u32[]{:S(2)}) copy-start(f32[32,128]{1,0:T(8,128)} %get-tuple-element.25) | copy-start | bytes 49156

commit v2 on v1

--- a/solution.py
+++ b/solution.py
@@ -15,6 +15,7 @@
 REST = NE - EARLY
 LATE = 512
 GROUP = 512
+CLASSES = 4
 ROWS = 32
 LANES = 128
 CELLS = ROWS * LANES
@@ -76,6 +77,7 @@
     late_maps,
     coupled,
     beside,
+    split,
     partial,
     outgoing,
     halo,
@@ -154,11 +156,14 @@
 
     no_edges = (jnp.zeros((NB, LANES), F32),) * 2
 
-    def send_blocks(source, target_ref, sent_sem, got_sem):
+    def position(device):
+        return lax.rem(device, CLASSES) * (devices // CLASSES) + lax.div(device, CLASSES)
+
+    def send_class(shift, source, target_ref, sent_sem, got_sem):
         def one(k, carry):
-            to = lax.rem(me + k, devices)
+            to = lax.rem(me + shift + CLASSES * k, devices)
             pltpu.make_async_remote_copy(
-                src_ref=source.at[to],
+                src_ref=source.at[position(to)],
                 dst_ref=target_ref.at[me],
                 send_sem=sent_sem,
                 recv_sem=got_sem,
@@ -167,7 +172,11 @@
             ).start()
             return carry
 
-        lax.fori_loop(1, devices, one, 0)
+        lax.fori_loop(1 if shift == 0 else 0, devices // CLASSES, one, 0)
+
+    def send_blocks(*where):
+        for shift in range(CLASSES):
+            send_class(shift, *where)
 
     def wait_blocks(source, target_ref, sent_sem, got_sem):
         all_but_one = pl.ds(0, devices - 1)
@@ -182,15 +191,11 @@
         everything.wait_recv()
         everything.wait_send()
 
-    def pack(source, out, first, last):
-        def one(m, carry):
-            at = pl.ds(pl.multiple_of(m * GROUP, GROUP), GROUP)
-            found = dot_nt(picker[at, :], source[...]).astype(BF16)
-            blocks = pl.ds(pl.multiple_of(m * (GROUP // CAP), GROUP // CAP), GROUP // CAP)
-            out[blocks, :, :] = found.reshape(GROUP // CAP, CAP, source.shape[0])
-            return carry
-
-        lax.fori_loop(first, last, one, 0)
+    def pack(m, source, out):
+        at = pl.ds(pl.multiple_of(m * GROUP, GROUP), GROUP)
+        found = dot_nt(picker[at, :], source[...]).astype(BF16)
+        blocks = pl.ds(pl.multiple_of(m * (GROUP // CAP), GROUP // CAP), GROUP // CAP)
+        out[blocks, :, :] = found.reshape(GROUP // CAP, CAP, source.shape[0])
 
     def state_layout():
         step = 1024
@@ -215,7 +220,8 @@
             hot = jnp.where((owner == owner_iota) & (flag > 0), 1.0, 0.0)
             counts = dot(hot.astype(BF16), tri)
             rank = jnp.sum(hot * (counts[:, :LANES] + before), axis=0, keepdims=True).astype(jnp.int32)
-            slots[i : i + 1, :] = jnp.where(flag > 0, owner * CAP + rank, -1)
+            place_of = (owner & (CLASSES - 1)) * (devices // CLASSES) + lax.shift_right_logical(owner, 2)
+            slots[i : i + 1, :] = jnp.where(flag > 0, place_of * CAP + rank, -1)
             before = before + counts[:, LANES:]
 
     def build_picker():
@@ -236,10 +242,18 @@
     def between(turn):
         if turn == 0:
             build_picker()
-            pack(early, sent_early, 0, picker.shape[0] // GROUP)
+
+            def one(m, carry):
+                pack(m, early, sent_early)
+                return carry
+
+            lax.fori_loop(0, CLASSES, one, 0)
         else:
             send_blocks(sent_early, moved_early, early_send, early_recv)
 
+    inverse = inverse_ref[...]
+    inverse_high = inverse.astype(BF16).astype(F32)
+    split[...] = jnp.concatenate([inverse_high, inverse_high, inverse - inverse_high], axis=1).astype(BF16)
     coupled[...] = jnp.zeros_like(coupled)
     for d in range(4):
         coupled[:, d * LANES : d * LANES + NB] = coupling_ref[d].astype(BF16)
@@ -282,7 +296,7 @@
             joined = jnp.concatenate(sums, axis=1)
             high = joined.astype(BF16)
             low = (joined - high.astype(F32)).astype(BF16)
-            product = dot(inverse_ref[...], jnp.concatenate([high, low, high], axis=0))
+            product = dot(split[...], jnp.concatenate([high, low, high], axis=0))
             for k in range(4):
                 i = g * 4 + k
                 values = product[:, k * LANES : (k + 1) * LANES] * scale_ref[i : i + 1, :]
@@ -321,10 +335,11 @@
         late[REST + 3 * NB : REST + 4 * NB, at] = jnp.where(lane == 0, near, own).astype(BF16)
         own = late[REST + 4 * NB : REST + 5 * NB, at].astype(F32)
         late[REST + 4 * NB : REST + 5 * NB, at] = jnp.where(lane == LANES - 1, far, own).astype(BF16)
-    pack(late, sent_late, 0, picker.shape[0] // GROUP)
-    send_blocks(sent_late, moved_late, late_send, late_recv)
-    own_early = pltpu.make_async_copy(sent_early.at[me], moved_early.at[me], self_sem.at[0])
-    own_late = pltpu.make_async_copy(sent_late.at[me], moved_late.at[me], self_sem.at[1])
+    for shift in range(CLASSES):
+        pack(lax.rem(me + shift, CLASSES), late, sent_late)
+        send_class(shift, sent_late, moved_late, late_send, late_recv)
+    own_early = pltpu.make_async_copy(sent_early.at[position(me)], moved_early.at[me], self_sem.at[0])
+    own_late = pltpu.make_async_copy(sent_late.at[position(me)], moved_late.at[me], self_sem.at[1])
     own_early.start()
     own_late.start()
 
@@ -356,7 +371,9 @@
     wait_blocks(sent_late, moved_late, late_send, late_recv)
 
 
-def owner_kernel(early_ref, late_ref, weights_ref, raised_ref, adjoint_ref):
+def owner_kernel(early_ref, late_ref, weights_ref, trace_ref, means_ref, raised_ref, adjoint_ref, final_ref, indicator_ref):
+    final_ref[...] = trace_ref[...]
+    indicator_ref[...] = means_ref[...]
     part = raised_ref.shape[1]
     early = early_ref[...].reshape(part, EARLY)
     late = late_ref[...].reshape(part, LATE)
@@ -391,9 +408,6 @@
 ):
     devices = n_px * n_py
     slots = devices * CAP
-    inverse_high = block_inverse.astype(BF16)
-    inverse_low = (block_inverse - inverse_high.astype(F32)).astype(BF16)
-    inverse_split = jnp.concatenate([inverse_high, inverse_high, inverse_low], axis=1)
     final_trace, indicator, moved_early, moved_late, weights = pl.pallas_call(
         functools.partial(main_kernel, n_px, n_py),
         out_shape=(
@@ -416,6 +430,7 @@
             pltpu.VMEM((LATE, NE_HI), BF16),
             pltpu.VMEM((NB, 4 * LANES), BF16),
             pltpu.VMEM((4 * LANES, CELLS), BF16),
+            pltpu.VMEM((NB, 3 * NB), BF16),
             pltpu.VMEM((ROWS, NB, LANES), F32),
             pltpu.VMEM((3, 4, NB, LANES), BF16),
             pltpu.VMEM((3, 4, NB, LANES), BF16),
@@ -439,7 +454,7 @@
         trace_rhs.reshape(NB * ROWS, LANES),
         face_scale,
         coupling,
-        inverse_split,
+        block_inverse,
         recover_self.T,
         jnp.transpose(recover_faces, (0, 2, 1)).reshape(NF, NE_HI),
         residual_map,
@@ -448,18 +463,28 @@
     )
 
     part = 32
-    raised_state, moved_adjoint = pl.pallas_call(
+    steps = devices // part
+    passed = (
+        pl.BlockSpec((NB * ROWS // steps, LANES), lambda i: (i, 0)),
+        pl.BlockSpec((ROWS // steps, LANES), lambda i: (i, 0)),
+    )
+    raised_state, moved_adjoint, final_trace, indicator = pl.pallas_call(
         owner_kernel,
-        out_shape=(jax.ShapeDtypeStruct((NE_HI, slots), BF16),) * 2,
-        grid=(devices // part,),
+        out_shape=(jax.ShapeDtypeStruct((NE_HI, slots), BF16),) * 2
+        + (
+            jax.ShapeDtypeStruct((NB * ROWS, LANES), F32),
+            jax.ShapeDtypeStruct((ROWS, LANES), F32),
+        ),
+        grid=(steps,),
         in_specs=[
             pl.BlockSpec((part, CAP, EARLY), lambda i: (i, 0, 0)),
             pl.BlockSpec((part, CAP, LATE), lambda i: (i, 0, 0)),
             pl.BlockSpec(weights.shape, lambda i: (0, 0), pipeline_mode=pl.Buffered(1)),
+            *passed,
         ],
-        out_specs=(pl.BlockSpec((NE_HI, part * CAP), lambda i: (0, i)),) * 2,
+        out_specs=(pl.BlockSpec((NE_HI, part * CAP), lambda i: (0, i)),) * 2 + passed,
         name="owner",
-    )(moved_early, moved_late, weights)
+    )(moved_early, moved_late, weights, final_trace, indicator)
     return (final_trace.reshape(NB, ROWS, LANES), indicator, raised_state, moved_adjoint)
 
 

time: 100 us -> 93 us (0.930)
  Pallas kernels: 95.3 us -> 91.8 us
  local copies, waits for them, and re-layouts: 1.67 us -> 0 us
  other arithmetic: 1.57 us -> 0 us
    pallas_call x1, Pallas kernels: 88.3 us -> 84 us  [per_device(): pl.pallas_call(functools.partial(main_kernel, n_px, n_py), out_shape=(jax...]
    unnamed x6 -> x0, local copies, waits for them, and re-layouts: 1.67 us -> none
where the time goes in v2:
time: 93 us; the launch traced here: 92.6 us
  Pallas kernels  91.8 us (99%)
    pallas_call x1, Pallas kernels, per_device(): pl.pallas_call(functools.partial(main_kernel, n_px, n_py), out_shape=(jax...  84 us
    pallas_call x1, Pallas kernels, per_device(): pl.pallas_call(owner_kernel, out_shape=(jax.ShapeDtypeStruct((NE_HI, slot...  7.84 us

profile of v2, /device:TPU:1, one launch (start us, length us, event | category | flops | bytes accessed | tf_op | source)
XLA Modules:
  0.0 92.6 jit_solution(7910202193576429364)
XLA Ops:
  0.6 84.0 %main.1 = (f32[2560,128]{1,0:T(8,128)}, f32[32,128]{1,0:T(8,128)}, bf16[128,16,256]{2,1,0:T(8,128)(2,1)}, bf16[128,16,512]{2,1,0:T(8,128)(2,1)}, bf16[640,1152]{1,0:T(8,128)(2,1)}) custom-call(bf16[10240,128]{1,0:T(8,128)(2,1)} %bitcast.10, s32[32,128]{1,0:T(8,128)} %owner_ref.1, s32[32,128]{1,0:T(8,128)} %flag_ref.1, f32[2560,128]{1,0:T(8,128)} %bitcast.11, ...), custom_call_target="tpu_custom_call" | custom-call | tf_op jit(solution)/shard_map/main/pallas_call | solution.py:411
  84.6 7.8 %owner.1 = (bf16[640,2048]{1,0:T(8,128)(2,1)}, bf16[640,2048]{1,0:T(8,128)(2,1)}, f32[2560,128]{1,0:T(8,128)}, f32[32,128]{1,0:T(8,128)}) custom-call(bf16[128,16,256]{2,1,0:T(8,128)(2,1)} %get-tuple-element.13.early_ref, bf16[128,16,512]{2,1,0:T(8,128)(2,1)} %get-tuple-element.14.late_ref, bf16[640,1152]{1,0:T(8,128)(2,1)} %get-tuple-element.15.weights_ref, ...), custom_call_target="tpu_custom_call" | custom-call | tf_op jit(solution)/shard_map/owner/pallas_call | solution.py:471

commit v3 on v2

--- a/solution.py
+++ b/solution.py
@@ -174,10 +174,6 @@
 
         lax.fori_loop(1 if shift == 0 else 0, devices // CLASSES, one, 0)
 
-    def send_blocks(*where):
-        for shift in range(CLASSES):
-            send_class(shift, *where)
-
     def wait_blocks(source, target_ref, sent_sem, got_sem):
         all_but_one = pl.ds(0, devices - 1)
         everything = pltpu.make_async_remote_copy(
@@ -242,14 +238,13 @@
     def between(turn):
         if turn == 0:
             build_picker()
-
-            def one(m, carry):
-                pack(m, early, sent_early)
-                return carry
-
-            lax.fori_loop(0, CLASSES, one, 0)
+            for shift in range(CLASSES):
+                pack(lax.rem(me + shift, CLASSES), early, sent_early)
+                if shift < CLASSES // 2:
+                    send_class(shift, sent_early, moved_early, early_send, early_recv)
         else:
-            send_blocks(sent_early, moved_early, early_send, early_recv)
+            for shift in range(CLASSES // 2, CLASSES):
+                send_class(shift, sent_early, moved_early, early_send, early_recv)
 
     inverse = inverse_ref[...]
     inverse_high = inverse.astype(BF16).astype(F32)

time: 93 us -> 98 us (1.054)
  Pallas kernels: 91.8 us -> 97.1 us
    pallas_call x1, Pallas kernels: 84 us -> 89.3 us  [per_device(): pl.pallas_call(functools.partial(main_kernel, n_px, n_py), out_shape=(jax...]
where the time goes in v3:
time: 98 us; the launch traced here: 97.9 us
  Pallas kernels  97.1 us (99%)
    pallas_call x1, Pallas kernels, per_device(): pl.pallas_call(functools.partial(main_kernel, n_px, n_py), out_shape=(jax...  89.3 us
    pallas_call x1, Pallas kernels, per_device(): pl.pallas_call(owner_kernel, out_shape=(jax.ShapeDtypeStruct((NE_HI, slot...  7.84 us

profile of v3, /device:TPU:1, one launch (start us, length us, event | category | flops | bytes accessed | tf_op | source)
XLA Modules:
  0.0 97.9 jit_solution(6015023174037386976)
XLA Ops:
  0.6 89.3 %main.1 = (f32[2560,128]{1,0:T(8,128)}, f32[32,128]{1,0:T(8,128)}, bf16[128,16,256]{2,1,0:T(8,128)(2,1)}, bf16[128,16,512]{2,1,0:T(8,128)(2,1)}, bf16[640,1152]{1,0:T(8,128)(2,1)}) custom-call(bf16[10240,128]{1,0:T(8,128)(2,1)} %bitcast.10, s32[32,128]{1,0:T(8,128)} %owner_ref.1, s32[32,128]{1,0:T(8,128)} %flag_ref.1, f32[2560,128]{1,0:T(8,128)} %bitcast.11, ...), custom_call_target="tpu_custom_call" | custom-call | tf_op jit(solution)/shard_map/main/pallas_call | solution.py:406
  89.9 7.8 %owner.1 = (bf16[640,2048]{1,0:T(8,128)(2,1)}, bf16[640,2048]{1,0:T(8,128)(2,1)}, f32[2560,128]{1,0:T(8,128)}, f32[32,128]{1,0:T(8,128)}) custom-call(bf16[128,16,256]{2,1,0:T(8,128)(2,1)} %get-tuple-element.13.early_ref, bf16[128,16,512]{2,1,0:T(8,128)(2,1)} %get-tuple-element.14.late_ref, bf16[640,1152]{1,0:T(8,128)(2,1)} %get-tuple-element.15.weights_ref, ...), custom_call_target="tpu_custom_call" | custom-call | tf_op jit(solution)/shard_map/owner/pallas_call | solution.py:466
